TPU v7x, 32 devices: a whole 2x2x4 slice. The times are simulated.
32 devices in a mesh: groups: 2 (over y), blk: 4 (over z), dp: 2 (over x), sub: 2 (over core).
Axes of the slice: x: 2, y: 2, z: 4, core: 2. Of those that a mesh axis runs over, the one named last changes fastest.
Arguments:
- view_a: bfloat16 [2048, 256], P(('groups', 'blk', 'dp', 'sub')), parts along dimension 0, may hold values from -6 to 6
- view_b: bfloat16 [2048, 256], P(('groups', 'blk', 'dp', 'sub')), parts along dimension 0, may hold values from -6 to 6
- prototypes: bfloat16 [32768, 256], P('blk'), may hold values from -6 to 6
- tile_mask: int32 [16, 256], replicated, may hold values from 0 to 1, as said below
- tile_region: int32 [32], P('groups'), parts along dimension 0, may hold values from 0 to 15, as said below
Outputs:
- grad_view_b: float32 [2048, 256], P(('groups', 'blk', 'dp', 'sub')), parts along dimension 0
- grad_prototypes: float32 [65536, 256], P(('groups', 'blk', 'dp', 'sub')), parts along dimension 0
There are 2 independent parts, one for each index of `groups`. A program takes and returns all parts, laid end to end along the dimension named above; an argument that names none is the same for every part. Nothing has to cross between parts.
Inputs may be any that keep to these rules, and one draw needn't show every extreme that they name: `tile_mask`: every prototype tile is 1 for at least one region, and every region for at least 16 tiles. `tile_region`: every region is named by at least one hit tile.
All inputs are finite; a program needn't handle non-finite values.
Results may differ from a plain program's by a relative error of at most 0.00045.
The roundings to bfloat16 on the way count: a program that leaves them out, or rounds other values in their place, can miss the bound.
Values may be sent and summed in bfloat16 or wider, within the bound.
A program may use at most 64 MiB of HBM per device.

v0:
```python
import jax
import jax.numpy as jnp
from jax import lax
from jax.sharding import PartitionSpec as P

TILE = 128
ITERS = 3
SOFTMAX_TEMPER = 0.1
EPSILON = 0.05
PART = ("blk", "dp", "sub")


def unit_rows(matrix):
    values = matrix.astype(jnp.float32)
    return (values * lax.rsqrt(jnp.sum(values * values, axis=1, keepdims=True) + 1e-06)).astype(
        jnp.bfloat16
    )


def body(view_a, view_b, prototypes, tile_mask, tile_region):
    n_dp = lax.axis_size("dp")
    n_sub = lax.axis_size("sub")
    blk_pos = lax.axis_index("blk")
    inner_pos = lax.axis_index("dp") * n_sub + lax.axis_index("sub")
    hit_dev, width = view_a.shape
    cols = prototypes.shape[0] // (n_dp * n_sub)
    tiles = cols // TILE
    regions = tile_mask.shape[0]
    protos = unit_rows(lax.dynamic_slice_in_dim(prototypes, inner_pos * cols, cols, 0))
    both = jnp.concatenate([unit_rows(view_a), unit_rows(view_b)], axis=1)
    both = lax.all_gather(both, PART, axis=0, tiled=True)
    rows_a, rows_b = (both[:, :width], both[:, width:])
    hits = rows_a.shape[0]
    own_tile = (blk_pos * n_dp * n_sub + inner_pos) * tiles
    my_mask = lax.dynamic_slice_in_dim(tile_mask, own_tile, tiles, 1).astype(jnp.float32)
    onehot = (tile_region[:, None] == jnp.arange(regions, dtype=jnp.int32)[None, :]).astype(
        jnp.float32
    )
    flags = jnp.dot(onehot, my_mask) > 0.5
    active = jnp.broadcast_to(
        flags[:, None, :, None], (hits // hit_dev, hit_dev, tiles, TILE)
    ).reshape(hits, cols)

    def scores(rows):
        return jnp.einsum("rd,kd->rk", rows, protos, preferred_element_type=jnp.float32)

    code_exp = jnp.where(active, jnp.exp((scores(rows_a) - 1.0) / EPSILON), 0.0).astype(
        jnp.bfloat16
    )
    pred = jnp.where(active, jnp.exp((scores(rows_b) - 1.0) / SOFTMAX_TEMPER), 0.0)
    norm = jnp.sum(pred, axis=1)
    code = code_exp.astype(jnp.float32)
    row = jnp.ones((hits,), jnp.float32)
    for sweep in range(ITERS):
        col = 1.0 / jnp.sum(code * row[:, None], axis=0)
        part = jnp.sum(code * col[None, :], axis=1)
        if sweep == 0:
            part, norm = lax.psum((part, norm), PART)
        else:
            part = lax.psum(part, PART)
        row = 1.0 / part
    grad = ((pred / norm[:, None] - row[:, None] * code * col[None, :]) / SOFTMAX_TEMPER).astype(
        jnp.bfloat16
    )
    hit_part = jnp.dot(grad, protos, preferred_element_type=jnp.float32)
    grad_protos = jnp.einsum("rk,rd->kd", grad, rows_b, preferred_element_type=jnp.float32)
    return (lax.psum_scatter(hit_part, PART, scatter_dimension=0, tiled=True), grad_protos)


def solution(mesh):
    spread = P(("groups", "blk", "dp", "sub"), None)
    return jax.shard_map(
        body,
        mesh=mesh,
        in_specs=(spread, spread, P("blk", None), P(), P("groups")),
        out_specs=(spread, spread),
        check_vma=False,
    )
```

profile of v0, /device:TPU:0, one launch (start us, length us, event | category | flops | bytes accessed | tf_op | source)
XLA Modules:
  0.0 244.8 jit_solution(6231227928295905269)
XLA Ops:
  7.2 0.0 all-gather.2.cloned.1.call-start
  7.2 0.9 fusion.17
  8.1 0.9 fusion.19
  9.0 0.9 fusion.18
  9.9 0.6 pad_maximum_fusion
  10.5 0.0 all-gather.2.cloned.1.call-update
  10.5 0.0 reduce-scatter.2.cloned.1.call-start
  10.6 1.6 fusion.10
  12.2 0.9 convolution_compare_fusion
  13.1 38.3 %all-gather.2.cloned.1.call-done = bf16[1024,512]{1,0:T(8,128)(2,1)} async-done(((bf16[64,512]{1,0:T(8,128)(2,1)}), bf16[1024,512]{1,0:T(8,128)(2,1)}) %all-gather.2.cloned.1.call-update) | async-done | bytes 1048592 | tf_op jit(solution)/shard_map/all_gather | solution.py:31
  51.4 0.6 broadcast_in_dim.6
  52.0 4.3 %convert_reduce_fusion = (f32[2048]{0:T(1024)S(1)}, bf16[1024,2048]{1,0:T(8,128)(2,1)S(1)}) fusion(f32[2048]{0:T(1024)S(1)} %add_rsqrt_fusion, bf16[8192,256]{1,0:T(8,128)(2,1)} %param.7, s32[]{:T(128)S(6)} %select_n.14, bf16[1024,512]{1,0:T(8,128)(2,1)} %all-gather.2.cloned.1.call-done, pred[128,8,16,128]{3,2,1,0:T(8,128)(4,1)S(1)} %bitcast.11), kind=kOutput, calls=%fused_computation.6 | convolution fusion | flops 1087895552 | bytes 7880708 | tf_op jit(solution)/shard_map/rd,kd->rk/dot_general | solution.py:45
  56.3 0.0 copy-start
  56.4 2.0 copy-done
  58.3 0.9 fusion
  59.2 31.6 %psum.29 = f32[1024]{0:T(1024)S(1)} all-reduce(f32[1024]{0:T(1024)S(1)} %fusion), channel_id=1, replica_groups=mesh['groups'=2,'blk'=4,'dp'=2,'sub'=2] {'blk','dp','sub'}, use_global_device_ids=true, to_apply=%region_7.8 | all-reduce | flops 1024 | bytes 8192 | tf_op jit(solution)/shard_map/psum | solution.py:58
  90.8 0.0 copy-start.2
  90.8 3.2 %fusion.1 = f32[2048]{0:T(1024)S(1)} fusion(bf16[1024,2048]{1,0:T(8,128)(2,1)} %copy-done, f32[1024]{0:T(1024)S(1)} %broadcast_divide_fusion.5), kind=kLoop, calls=%fused_computation.8 | loop fusion | flops 6289408 | bytes 4206592 | tf_op jit(solution)/shard_map/reduce_sum | solution.py:55
  94.0 3.1 %fusion.2 = f32[1024]{0:T(1024)S(1)} fusion(bf16[1024,2048]{1,0:T(8,128)(2,1)} %copy-done, f32[2048]{0:T(1024)S(1)} %broadcast_divide_fusion.1), kind=kLoop, calls=%fused_computation.9 | loop fusion | flops 6290432 | bytes 4206592 | tf_op jit(solution)/shard_map/reduce_sum | solution.py:56
  97.1 29.7 %psum.30 = f32[1024]{0:T(1024)S(1)} all-reduce(f32[1024]{0:T(1024)S(1)} %fusion.2), channel_id=1, replica_groups=mesh['groups'=2,'blk'=4,'dp'=2,'sub'=2] {'blk','dp','sub'}, use_global_device_ids=true, to_apply=%region_10.11 | all-reduce | flops 1024 | bytes 8192 | tf_op jit(solution)/shard_map/psum | solution.py:60
  126.8 3.1 %fusion.3 = f32[2048]{0:T(1024)S(1)} fusion(bf16[1024,2048]{1,0:T(8,128)(2,1)} %copy-done, f32[1024]{0:T(1024)S(1)} %broadcast_divide_fusion.4), kind=kLoop, calls=%fused_computation.10 | loop fusion | flops 6289408 | bytes 4206592 | tf_op jit(solution)/shard_map/reduce_sum | solution.py:55
  129.9 3.1 %fusion.4 = f32[1024]{0:T(1024)S(1)} fusion(bf16[1024,2048]{1,0:T(8,128)(2,1)} %copy-done, f32[2048]{0:T(1024)S(1)} %broadcast_divide_fusion), kind=kLoop, calls=%fused_computation.11 | loop fusion | flops 6290432 | bytes 4206592 | tf_op jit(solution)/shard_map/reduce_sum | solution.py:56
  132.9 0.0 copy-done.2
  132.9 7.3 %fusion.9 = (f32[1024]{0:T(1024)S(1)}, f32[1024,2048]{1,0:T(8,128)}) fusion(pred[128,8,16,128]{3,2,1,0:T(8,128)(4,1)S(1)} %bitcast.12, f32[2048]{0:T(1024)S(1)} %add_rsqrt_fusion, bf16[8192,256]{1,0:T(8,128)(2,1)} %param.7, s32[]{:T(128)S(6)} %select_n.14, bf16[1024,512]{1,0:T(8,128)(2,1)S(1)} %copy-done.2), kind=kOutput, calls=%fused_computation.18 | convolution fusion | flops 1083702272 | bytes 12070916 | tf_op jit(solution)/shard_map/rd,kd->rk/dot_general | solution.py:45
  140.2 30.0 %all-reduce = (f32[1024]{0:T(1024)S(1)}, f32[1024]{0:T(1024)S(1)}) all-reduce(f32[1024]{0:T(1024)S(1)} %fusion.4, f32[1024]{0:T(1024)S(1)} %get-tuple-element.6), channel_id=1, replica_groups=mesh['groups'=2,'blk'=4,'dp'=2,'sub'=2] {'blk','dp','sub'}, use_global_device_ids=true, to_apply=%region_13.14 | all-reduce | flops 2048 | bytes 16384 | tf_op jit(solution)/shard_map/psum | solution.py:60
  170.2 7.4 %fusion.8 = bf16[1024,2048]{1,0:T(8,128)(2,1)S(1)} fusion(bf16[1024,2048]{1,0:T(8,128)(2,1)} %copy-done, f32[1024,2048]{1,0:T(8,128)} %get-tuple-element.7, pred[128,8,16,128]{3,2,1,0:T(8,128)(4,1)S(1)} %bitcast.13, f32[1024]{0:T(1024)S(1)} %broadcast_divide_fusion.3, f32[2048]{0:T(1024)S(1)} %broadcast_divide_fusion, f32[1024]{0:T(1024)S(1)} %get-tuple-element.3), kind=kLoop, calls=%fused_computation.15 | loop fusion | flops 20971520 | bytes 18890752 | tf_op jit(solution)/shard_map/convert_element_type | solution.py:62
  177.6 0.0 copy-start.1
  177.7 1.9 copy-done.1
  179.6 3.6 %fusion.25 = f32[1024,256]{1,0:T(8,128)} fusion(bf16[1024,2048]{1,0:T(8,128)(2,1)S(1)} %fusion.8, f32[2048]{0:T(1024)S(1)} %add_rsqrt_fusion, bf16[8192,256]{1,0:T(8,128)(2,1)} %param.7, s32[]{:T(128)S(6)} %select_n.14), kind=kOutput, calls=%fused_computation.52 | convolution fusion | flops 1075314688 | bytes 6299652 | tf_op jit(solution)/shard_map/dot_general | solution.py:65
  183.1 0.0 reduce-scatter.2.cloned.1.call-update
  183.2 4.8 %fusion.13 = f32[2048,256]{1,0:T(8,128)} fusion(bf16[1024,2048]{1,0:T(8,128)(2,1)} %copy-done.1, bf16[1024,512]{1,0:T(8,128)(2,1)S(1)} %copy-done.2), kind=kOutput, calls=%fused_computation.25 | convolution fusion | flops 1073741824 | bytes 6815744 | tf_op jit(solution)/shard_map/rk,rd->kd/dot_general | solution.py:66
  188.0 49.9 %reduce-scatter.2.cloned.1.call-done = f32[64,256]{1,0:T(8,128)} async-done(((f32[1024,256]{1,0:T(8,128)}), f32[64,256]{1,0:T(8,128)}) %reduce-scatter.2.cloned.1.call-update) | async-done | bytes 65552 | tf_op jit(solution)/shard_map/reduce_scatter | solution.py:67
  (9 shorter events, 0.0 us)
Async XLA Ops:
  7.2 44.2 %all-gather.2.cloned.1.call-start = ((), (), s32[]{:S(2)}) async-start(), calls=%async_computation.1 | async-start | bytes 1114112 | tf_op jit(solution)/shard_map/all_gather | solution.py:31
  10.5 227.4 %reduce-scatter.2.cloned.1.call-start = ((), (), s32[]{:S(2)}) async-start(), calls=%async_computation.2 | async-start | bytes 1114112 | tf_op jit(solution)/shard_map/reduce_scatter | solution.py:67
  56.3 2.0 copy-start
  90.8 42.1 %copy-start.2 = (bf16[1024,512]{1,0:T(8,128)(2,1)S(1)}, bf16[1024,512]{1,0:T(8,128)(2,1)}, u32[]{:S(2)}) copy-start(bf16[1024,512]{1,0:T(8,128)(2,1)} %all-gather.2.cloned.1.call-done) | copy-start | bytes 3145732
  177.6 1.9 copy-start.1
Sparse Core Ops, SparseCore 0:
  10.7 40.6 all-gather.1
  183.3 54.6 reduce-scatter.1
where the time goes:
time: 245 us
  blocking collectives  91.2 us (37%)
  waiting for transfers between devices  88.3 us (36%)
  other arithmetic  25.6 us (10%)
  matrix products  20.9 us (9%)
  between operations  14.2 us (6%)
  local copies, waits for them, and re-layouts  4.48 us (2%)
    psum x2, blocking collectives, body(): part = lax.psum(part, PART)  59.6 us
    reduce_scatter x1, waiting for transfers between devices, body(): lax.psum_scatter(hit_part, PART, scatter_dimension=0, tiled=True)  49.9 us
    all_gather x1, waiting for transfers between devices, body(): both = lax.all_gather(both, PART, axis=0, tiled=True)  38.3 us
    psum x1, blocking collectives, body(): part, norm = lax.psum((part, norm), PART)  31.6 us
    dot_general x2, matrix products, scores(): jnp.einsum('rd,kd->rk', rows, protos, preferred_element_type=jnp.float32)  11.6 us
    convert_element_type x1, other arithmetic, body(): ((pred / norm[:, None] - row[:, None] * code * col[None, :]) / SOFTMAX_TE...  7.44 us
    reduce_sum x3, other arithmetic, body(): part = jnp.sum(code * col[None, :], axis=1)  7.06 us
    reduce_sum x2, other arithmetic, body(): col = 1.0 / jnp.sum(code * row[:, None], axis=0)  6.24 us
  transfers between devices with their start and end apart: 2, of which 2 were waited for; matrix products, arithmetic and copies ran while one was open for 3% of the time, Pallas kernels for 0%

commit v1 on v0

--- a/solution.py
+++ b/solution.py
@@ -57,7 +57,8 @@
         if sweep == 0:
             part, norm = lax.psum((part, norm), PART)
         else:
-            part = lax.psum(part, PART)
+            shards = lax.all_gather(part, PART)
+            part = jnp.sum(shards, axis=0)
         row = 1.0 / part
     grad = ((pred / norm[:, None] - row[:, None] * code * col[None, :]) / SOFTMAX_TEMPER).astype(
         jnp.bfloat16

time: 245 us -> 222 us (0.906)
  blocking collectives: 91.2 us -> 68.8 us
    psum x2 -> x0, blocking collectives: 59.6 us -> none  [body(): part = lax.psum(part, PART)]
    all_gather x0 -> x2, blocking collectives: none -> 36.7 us  [body(): shards = lax.all_gather(part, PART)]
where the time goes in v1:
time: 222 us; the launch traced here: 221 us
  waiting for transfers between devices  88.3 us (40%)
  blocking collectives  68.8 us (31%)
  other arithmetic  25.5 us (11%)
  matrix products  21.5 us (10%)
  between operations  14.2 us (6%)
  local copies, waits for them, and re-layouts  2.57 us (1%)
    reduce_scatter x1, waiting for transfers between devices, body(): lax.psum_scatter(hit_part, PART, scatter_dimension=0, tiled=True)  49.9 us
    all_gather x1, waiting for transfers between devices, body(): both = lax.all_gather(both, PART, axis=0, tiled=True)  38.3 us
    all_gather x2, blocking collectives, body(): shards = lax.all_gather(part, PART)  36.7 us
    psum x1, blocking collectives, body(): part, norm = lax.psum((part, norm), PART)  32.1 us
    dot_general x2, matrix products, scores(): jnp.einsum('rd,kd->rk', rows, protos, preferred_element_type=jnp.float32)  12.2 us
    convert_element_type x1, other arithmetic, body(): ((pred / norm[:, None] - row[:, None] * code * col[None, :]) / SOFTMAX_TE...  7.44 us
    reduce_sum x3, other arithmetic, body(): part = jnp.sum(code * col[None, :], axis=1)  7.06 us
    reduce_sum x2, other arithmetic, body(): col = 1.0 / jnp.sum(code * row[:, None], axis=0)  6.15 us
  transfers between devices with their start and end apart: 2, of which 2 were waited for; matrix products, arithmetic and copies ran while one was open for 3% of the time, Pallas kernels for 0%

profile of v1, /device:TPU:0, one launch (start us, length us, event | category | flops | bytes accessed | tf_op | source)
XLA Modules:
  0.0 221.1 jit_solution(14893754254461348553)
XLA Ops:
  7.2 0.0 all-gather.4.cloned.1.call-start
  7.2 0.9 fusion.17
  8.1 0.9 fusion.19
  9.0 0.9 fusion.18
  9.9 0.6 pad_maximum_fusion
  10.5 0.0 all-gather.4.cloned.1.call-update
  10.5 0.0 reduce-scatter.2.cloned.1.call-start
  10.6 1.6 fusion.10
  12.2 0.9 convolution_compare_fusion
  13.1 38.3 %all-gather.4.cloned.1.call-done = bf16[1024,512]{1,0:T(8,128)(2,1)} async-done(((bf16[64,512]{1,0:T(8,128)(2,1)}), bf16[1024,512]{1,0:T(8,128)(2,1)}) %all-gather.4.cloned.1.call-update) | async-done | bytes 1048592 | tf_op jit(solution)/shard_map/all_gather | solution.py:31
  51.4 0.6 broadcast_in_dim.6
  52.0 0.0 copy-start.2
  52.0 4.4 %convert_reduce_fusion = (f32[2048]{0:T(1024)S(1)}, bf16[1024,2048]{1,0:T(8,128)(2,1)S(1)}) fusion(f32[2048]{0:T(1024)S(1)} %add_rsqrt_fusion, bf16[8192,256]{1,0:T(8,128)(2,1)} %param.7, s32[]{:T(128)S(6)} %select_n.14, bf16[1024,512]{1,0:T(8,128)(2,1)} %all-gather.4.cloned.1.call-done, pred[128,8,16,128]{3,2,1,0:T(8,128)(4,1)S(1)} %bitcast.11), kind=kOutput, calls=%fused_computation.6 | convolution fusion | flops 1087895552 | bytes 7880708 | tf_op jit(solution)/shard_map/rd,kd->rk/dot_general | solution.py:45
  56.4 0.0 copy-start
  56.5 0.9 fusion
  57.4 0.0 copy-done.2
  57.4 7.8 %fusion.9 = (f32[1024]{0:T(1024)S(1)}, f32[1024,2048]{1,0:T(8,128)}) fusion(pred[128,8,16,128]{3,2,1,0:T(8,128)(4,1)S(1)} %bitcast.12, f32[2048]{0:T(1024)S(1)} %add_rsqrt_fusion, bf16[8192,256]{1,0:T(8,128)(2,1)} %param.7, s32[]{:T(128)S(6)} %select_n.14, bf16[1024,512]{1,0:T(8,128)(2,1)S(1)} %copy-done.2), kind=kOutput, calls=%fused_computation.18 | convolution fusion | flops 1083702272 | bytes 12070916 | tf_op jit(solution)/shard_map/rd,kd->rk/dot_general | solution.py:45
  65.2 0.0 copy-done
  65.2 32.1 %all-reduce = (f32[1024]{0:T(1024)S(1)}, f32[1024]{0:T(1024)S(1)}) all-reduce(f32[1024]{0:T(1024)S(1)} %fusion, f32[1024]{0:T(1024)S(1)} %get-tuple-element.6), channel_id=1, replica_groups=mesh['groups'=2,'blk'=4,'dp'=2,'sub'=2] {'blk','dp','sub'}, use_global_device_ids=true, to_apply=%region_7.8 | all-reduce | flops 2048 | bytes 16384 | tf_op jit(solution)/shard_map/psum | solution.py:58
  97.3 3.1 %fusion.1 = f32[2048]{0:T(1024)S(1)} fusion(bf16[1024,2048]{1,0:T(8,128)(2,1)} %copy-done, f32[1024]{0:T(1024)S(1)} %broadcast_divide_fusion.5), kind=kLoop, calls=%fused_computation.8 | loop fusion | flops 6289408 | bytes 4206592 | tf_op jit(solution)/shard_map/reduce_sum | solution.py:55
  100.4 3.1 %fusion.2 = f32[1024]{0:T(1024)S(1)} fusion(bf16[1024,2048]{1,0:T(8,128)(2,1)} %copy-done, f32[2048]{0:T(1024)S(1)} %broadcast_divide_fusion.1), kind=kLoop, calls=%fused_computation.9 | loop fusion | flops 6290432 | bytes 4206592 | tf_op jit(solution)/shard_map/reduce_sum | solution.py:56
  103.4 17.5 %all-gather = f32[16384]{0:T(1024)S(1)} all-gather(f32[1024]{0:T(1024)S(1)} %fusion.2), channel_id=2, replica_groups=mesh['groups'=2,'blk'=4,'dp'=2,'sub'=2] {'blk','dp','sub'}, dimensions={0}, use_global_device_ids=true | all-gather | bytes 69632 | tf_op jit(solution)/shard_map/all_gather | solution.py:60
  121.0 3.1 %fusion.3 = f32[2048]{0:T(1024)S(1)} fusion(bf16[1024,2048]{1,0:T(8,128)(2,1)} %copy-done, f32[1024]{0:T(1024)S(1)} %broadcast_divide_fusion.4), kind=kLoop, calls=%fused_computation.10 | loop fusion | flops 6289408 | bytes 4206592 | tf_op jit(solution)/shard_map/reduce_sum | solution.py:55
  124.1 3.1 %fusion.4 = f32[1024]{0:T(1024)S(1)} fusion(bf16[1024,2048]{1,0:T(8,128)(2,1)} %copy-done, f32[2048]{0:T(1024)S(1)} %broadcast_divide_fusion), kind=kLoop, calls=%fused_computation.11 | loop fusion | flops 6290432 | bytes 4206592 | tf_op jit(solution)/shard_map/reduce_sum | solution.py:56
  127.1 19.2 %all-gather.1 = f32[16384]{0:T(1024)S(1)} all-gather(f32[1024]{0:T(1024)S(1)} %fusion.4), channel_id=3, replica_groups=mesh['groups'=2,'blk'=4,'dp'=2,'sub'=2] {'blk','dp','sub'}, dimensions={0}, use_global_device_ids=true | all-gather | bytes 69632 | tf_op jit(solution)/shard_map/all_gather | solution.py:60
  146.4 7.4 %fusion.8 = bf16[1024,2048]{1,0:T(8,128)(2,1)S(1)} fusion(bf16[1024,2048]{1,0:T(8,128)(2,1)} %copy-done, f32[1024,2048]{1,0:T(8,128)} %get-tuple-element.7, pred[128,8,16,128]{3,2,1,0:T(8,128)(4,1)S(1)} %bitcast.13, f32[1024]{0:T(1024)S(1)} %broadcast_divide_fusion.3, f32[2048]{0:T(1024)S(1)} %broadcast_divide_fusion, f32[1024]{0:T(1024)S(1)} %get-tuple-element.3), kind=kLoop, calls=%fused_computation.15 | loop fusion | flops 20971520 | bytes 18890752 | tf_op jit(solution)/shard_map/convert_element_type | solution.py:63
  153.9 0.0 copy-start.1
  153.9 1.9 copy-done.1
  155.8 3.6 %fusion.25 = f32[1024,256]{1,0:T(8,128)} fusion(bf16[1024,2048]{1,0:T(8,128)(2,1)S(1)} %fusion.8, f32[2048]{0:T(1024)S(1)} %add_rsqrt_fusion, bf16[8192,256]{1,0:T(8,128)(2,1)} %param.7, s32[]{:T(128)S(6)} %select_n.14), kind=kOutput, calls=%fused_computation.52 | convolution fusion | flops 1075314688 | bytes 6299652 | tf_op jit(solution)/shard_map/dot_general | solution.py:66
  159.4 0.0 reduce-scatter.2.cloned.1.call-update
  159.4 4.9 %fusion.13 = f32[2048,256]{1,0:T(8,128)} fusion(bf16[1024,2048]{1,0:T(8,128)(2,1)} %copy-done.1, bf16[1024,512]{1,0:T(8,128)(2,1)S(1)} %copy-done.2), kind=kOutput, calls=%fused_computation.25 | convolution fusion | flops 1073741824 | bytes 6815744 | tf_op jit(solution)/shard_map/rk,rd->kd/dot_general | solution.py:67
  164.3 49.9 %reduce-scatter.2.cloned.1.call-done = f32[64,256]{1,0:T(8,128)} async-done(((f32[1024,256]{1,0:T(8,128)}), f32[64,256]{1,0:T(8,128)}) %reduce-scatter.2.cloned.1.call-update) | async-done | bytes 65552 | tf_op jit(solution)/shard_map/reduce_scatter | solution.py:68
  (13 shorter events, 0.1 us)
Async XLA Ops:
  7.2 44.2 %all-gather.4.cloned.1.call-start = ((), (), s32[]{:S(2)}) async-start(), calls=%async_computation.1 | async-start | bytes 1114112 | tf_op jit(solution)/shard_map/all_gather | solution.py:31
  10.5 203.7 %reduce-scatter.2.cloned.1.call-start = ((), (), s32[]{:S(2)}) async-start(), calls=%async_computation.2 | async-start | bytes 1114112 | tf_op jit(solution)/shard_map/reduce_scatter | solution.py:68
  52.0 5.3 %copy-start.2 = (bf16[1024,512]{1,0:T(8,128)(2,1)S(1)}, bf16[1024,512]{1,0:T(8,128)(2,1)}, u32[]{:S(2)}) copy-start(bf16[1024,512]{1,0:T(8,128)(2,1)} %all-gather.4.cloned.1.call-done) | copy-start | bytes 3145732
  56.4 8.7 %copy-start = (bf16[1024,2048]{1,0:T(8,128)(2,1)}, bf16[1024,2048]{1,0:T(8,128)(2,1)S(1)}, u32[]{:S(2)}) copy-start(bf16[1024,2048]{1,0:T(8,128)(2,1)S(1)} %get-tuple-element.5) | copy-start | bytes 12582916
  153.9 1.9 copy-start.1
Sparse Core Ops, SparseCore 0:
  10.7 40.6 all-gather.3
  159.5 54.6 reduce-scatter.1
